TPU v7x, 32 devices: a whole 2x2x4 slice. The times are simulated.
32 devices in a mesh: blk: 16 (over z, y, x), col: 2 (over core).
Axes of the slice: x: 2, y: 2, z: 4, core: 2. Of those that a mesh axis runs over, the one named last changes fastest.
Arguments:
- queries: bfloat16 [128, 16384], P('blk', 'col'), may hold values from -6 to 6
- factor: bfloat16 [16384, 1024], P('col', 'blk'), may hold values from -0.046875 to 0.046875
- eigenvalues: float32 [1024], replicated, may hold values from 0.05 to 20
- damping: float32 [1], replicated, may hold values from 0.5 to 2
- train_rows: bfloat16 [16384, 16384], P('blk', 'col'), may hold values from -0.046875 to 0.046875
Outputs:
- scores: bfloat16 [128, 16384], P('col', 'blk')
All inputs are finite; a program needn't handle non-finite values.
Results may differ from a plain program's by a relative error of at most 0.0049.
Values may be sent and summed in bfloat16 or wider, within the bound.
A program may use at most 64 MiB of HBM per device.

v0:
```python
import jax
import jax.numpy as jnp
from jax import lax
from jax.sharding import PartitionSpec as P


def per_device(queries, factor, eigenvalues, damping, train_rows):
    damp_value = damping[0]
    weights = eigenvalues / (eigenvalues + damp_value)
    query_part = lax.all_to_all(queries, "blk", split_axis=1, concat_axis=0, tiled=True)
    factor_part = lax.all_to_all(factor, "blk", split_axis=0, concat_axis=1, tiled=True)
    partial_value = jnp.dot(query_part, factor_part, preferred_element_type=jnp.float32)
    coefficient = lax.psum(partial_value, ("blk", "col"))
    scaled = coefficient * weights[None, :]
    correction = jnp.dot(scaled, factor_part.astype(jnp.float32).T, precision=lax.Precision.HIGHEST)
    pre_part = ((query_part.astype(jnp.float32) - correction) / damp_value).astype(jnp.bfloat16)
    pre_all = lax.all_gather(pre_part, "blk", axis=1, tiled=True)
    partial_scores = jnp.einsum(
        "qk,nk->qn", pre_all, train_rows, preferred_element_type=jnp.float32
    )
    scores = lax.psum_scatter(partial_scores, "col", scatter_dimension=0, tiled=True)
    return scores.astype(jnp.bfloat16)


def solution(mesh):
    in_specs = (P("blk", "col"), P("col", "blk"), P(), P(), P("blk", "col"))
    out_specs = P("col", "blk")
    return jax.shard_map(
        per_device, mesh=mesh, in_specs=in_specs, out_specs=out_specs, check_vma=False
    )
```

profile of v0, /device:TPU:0, one launch (start us, length us, event | category | flops | bytes accessed | tf_op | source)
XLA Modules:
  0.0 269.8 jit_solution(12998497539709083565)
XLA Ops:
  6.5 8.3 %all-to-all-start = ((bf16[8,16,512]{2,0,1:T(8,128)(2,1)}), bf16[8,16,512]{2,0,1:T(8,128)(2,1)S(1)}, u32[]{:S(2)}, u32[]{:S(2)}) async-start(bf16[8,16,512]{2,0,1:T(8,128)(2,1)} %bitcast.25), calls=%async_computation | async-start | bytes 262144 | tf_op jit(solution)/shard_map/all_to_all | solution.py:10
  14.9 0.0 all-reduce.2.cloned.1.call-start
  14.9 1.3 copy.10
  16.3 6.4 %all-to-all-done = bf16[8,16,512]{2,0,1:T(8,128)(2,1)S(1)} async-done(((bf16[8,16,512]{2,0,1:T(8,128)(2,1)}), bf16[8,16,512]{2,0,1:T(8,128)(2,1)S(1)}, u32[]{:S(2)}, u32[]{:S(2)}) %all-to-all-start) | async-done | bytes 131104 | tf_op jit(solution)/shard_map/all_to_all | solution.py:10
  22.7 28.3 %all_to_all.38 = bf16[16,512,64]{1,2,0:T(8,128)(2,1)S(1)} all-to-all(bf16[16,512,64]{1,2,0:T(8,128)(2,1)S(1)} %bitcast.21), channel_id=1, replica_groups=mesh['blk'=16,'col'=2] {'blk'}, dimensions={0} | all-to-all | bytes 2097152 | tf_op jit(solution)/shard_map/all_to_all | solution.py:11
  51.0 1.3 fusion.4
  52.3 0.0 all-reduce.2.cloned.1.call-update
  52.3 0.0 all-gather.2.cloned.1.call-start
  53.0 0.7 add_divide_fusion
  53.7 126.2 %all-reduce.2.cloned.1.call-done = f32[128,1024]{1,0:T(8,128)} async-done(((f32[128,1024]{1,0:T(8,128)}), f32[128,1024]{1,0:T(8,128)}) %all-reduce.2.cloned.1.call-update) | async-done | bytes 524304 | tf_op jit(solution)/shard_map/psum | solution.py:13
  179.9 2.3 fusion.1
  182.2 0.0 all-gather.2.cloned.1.call-update
  182.2 0.0 reduce-scatter.2.cloned.1.call-start
  182.2 60.3 %all-gather.2.cloned.1.call-done = bf16[128,8192]{1,0:T(8,128)(2,1)} async-done(((bf16[128,512]{1,0:T(8,128)(2,1)}), bf16[128,8192]{1,0:T(8,128)(2,1)}) %all-gather.2.cloned.1.call-update) | async-done | bytes 2097168 | tf_op jit(solution)/shard_map/all_gather | solution.py:17
  242.5 12.9 %fusion.6 = f32[128,1024]{1,0:T(8,128)} fusion(bf16[128,8192]{1,0:T(8,128)(2,1)} %all-gather.2.cloned.1.call-done, bf16[1024,8192]{1,0:T(8,128)(2,1)} %param.9), kind=kOutput, calls=%fused_computation.9 | convolution fusion | flops 2147483648 | bytes 19398656 | tf_op jit(solution)/shard_map/qk,nk->qn/dot_general | solution.py:18
  255.4 0.0 reduce-scatter.2.cloned.1.call-update
  255.4 6.3 %reduce-scatter.2.cloned.1.call-done = f32[64,1024]{1,0:T(8,128)} async-done(((f32[128,1024]{1,0:T(8,128)}), f32[64,1024]{1,0:T(8,128)}) %reduce-scatter.2.cloned.1.call-update) | async-done | bytes 262160 | tf_op jit(solution)/shard_map/reduce_scatter | solution.py:21
  261.7 1.6 convert_element_type.12
Async XLA Ops:
  6.5 16.1 %all-to-all-start = ((bf16[8,16,512]{2,0,1:T(8,128)(2,1)}), bf16[8,16,512]{2,0,1:T(8,128)(2,1)S(1)}, u32[]{:S(2)}, u32[]{:S(2)}) async-start(bf16[8,16,512]{2,0,1:T(8,128)(2,1)} %bitcast.25), calls=%async_computation | async-start | bytes 262144 | tf_op jit(solution)/shard_map/all_to_all | solution.py:10
  14.9 165.0 %all-reduce.2.cloned.1.call-start = ((), (), s32[]{:S(2)}) async-start(), calls=%async_computation.3 | async-start | bytes 1048576 | tf_op jit(solution)/shard_map/psum | solution.py:13
  52.3 190.2 %all-gather.2.cloned.1.call-start = ((), (), s32[]{:S(2)}) async-start(), calls=%async_computation.4 | async-start | bytes 2228224 | tf_op jit(solution)/shard_map/all_gather | solution.py:17
  182.2 79.5 %reduce-scatter.2.cloned.1.call-start = ((), (), s32[]{:S(2)}) async-start(), calls=%async_computation.5 | async-start | bytes 786432 | tf_op jit(solution)/shard_map/reduce_scatter | solution.py:21
Sparse Core Ops, SparseCore 0:
  52.4 127.3 all-reduce.1
  182.6 59.8 all-gather.1
  255.6 6.0 reduce-scatter.1
where the time goes:
time: 270 us
  waiting for transfers between devices  199 us (74%)
  blocking collectives  28.3 us (10%)
  matrix products  16.4 us (6%)
  between operations  13.8 us (5%)
  starting transfers between devices  8.47 us (3%)
    psum x1, waiting for transfers between devices, per_device(): coefficient = lax.psum(partial_value, ('blk', 'col'))  126 us
    all_gather x1, waiting for transfers between devices, per_device(): pre_all = lax.all_gather(pre_part, 'blk', axis=1, tiled=True)  60.3 us
    all_to_all x1, blocking collectives, per_device(): lax.all_to_all(factor, 'blk', split_axis=0, concat_axis=1, tiled=True)  28.3 us
    dot_general x1, matrix products, per_device(): jnp.einsum('qk,nk->qn', pre_all, train_rows, preferred_element_type=jnp.f...  12.9 us
    all_to_all x1, starting transfers between devices, per_device(): lax.all_to_all(queries, 'blk', split_axis=1, concat_axis=0, tiled=True)  8.34 us
    all_to_all x1, waiting for transfers between devices, per_device(): lax.all_to_all(queries, 'blk', split_axis=1, concat_axis=0, tiled=True)  6.41 us
    reduce_scatter x1, waiting for transfers between devices, per_device(): lax.psum_scatter(partial_scores, 'col', scatter_dimension=0, tiled=True)  6.26 us
  transfers between devices with their start and end apart: 4, of which 4 were waited for; matrix products, arithmetic and copies ran while one was open for 1% of the time, Pallas kernels for 0%

commit v1 on v0

--- a/solution.py
+++ b/solution.py
@@ -10,7 +10,8 @@
     query_part = lax.all_to_all(queries, "blk", split_axis=1, concat_axis=0, tiled=True)
     factor_part = lax.all_to_all(factor, "blk", split_axis=0, concat_axis=1, tiled=True)
     partial_value = jnp.dot(query_part, factor_part, preferred_element_type=jnp.float32)
-    coefficient = lax.psum(partial_value, ("blk", "col"))
+    parts = lax.all_gather(partial_value, ("blk", "col"))
+    coefficient = jnp.sum(parts, axis=0)
     scaled = coefficient * weights[None, :]
     correction = jnp.dot(scaled, factor_part.astype(jnp.float32).T, precision=lax.Precision.HIGHEST)
     pre_part = ((query_part.astype(jnp.float32) - correction) / damp_value).astype(jnp.bfloat16)

time: 270 us -> 261 us (0.967)
  waiting for transfers between devices: 199 us -> 183 us
  other arithmetic: 2.31 us -> 9.77 us
    psum x1 -> x0, waiting for transfers between devices: 126 us -> none  [per_device(): coefficient = lax.psum(partial_value, ('blk', 'col'))]
    all_gather x0 -> x1, waiting for transfers between devices: none -> 111 us  [per_device(): parts = lax.all_gather(partial_value, ('blk', 'col'))]
    reduce_sum x0 -> x1, other arithmetic: none -> 7.45 us  [per_device(): coefficient = jnp.sum(parts, axis=0)]
where the time goes in v1:
time: 261 us; the launch traced here: 260 us
  waiting for transfers between devices  183 us (70%)
  blocking collectives  28.3 us (11%)
  matrix products  15.4 us (6%)
  between operations  13.8 us (5%)
  other arithmetic  9.77 us (4%)
  starting transfers between devices  8.47 us (3%)
    all_gather x1, waiting for transfers between devices, per_device(): parts = lax.all_gather(partial_value, ('blk', 'col'))  111 us
    all_gather x1, waiting for transfers between devices, per_device(): pre_all = lax.all_gather(pre_part, 'blk', axis=1, tiled=True)  59.2 us
    all_to_all x1, blocking collectives, per_device(): lax.all_to_all(factor, 'blk', split_axis=0, concat_axis=1, tiled=True)  28.3 us
    dot_general x1, matrix products, per_device(): jnp.einsum('qk,nk->qn', pre_all, train_rows, preferred_element_type=jnp.f...  12.9 us
    all_to_all x1, starting transfers between devices, per_device(): lax.all_to_all(queries, 'blk', split_axis=1, concat_axis=0, tiled=True)  8.34 us
    reduce_sum x1, other arithmetic, per_device(): coefficient = jnp.sum(parts, axis=0)  7.45 us
    all_to_all x1, waiting for transfers between devices, per_device(): lax.all_to_all(queries, 'blk', split_axis=1, concat_axis=0, tiled=True)  6.41 us
    reduce_scatter x1, waiting for transfers between devices, per_device(): lax.psum_scatter(partial_scores, 'col', scatter_dimension=0, tiled=True)  6.26 us
  transfers between devices with their start and end apart: 4, of which 4 were waited for; matrix products, arithmetic and copies ran while one was open for 1% of the time, Pallas kernels for 0%

profile of v1, /device:TPU:0, one launch (start us, length us, event | category | flops | bytes accessed | tf_op | source)
XLA Modules:
  0.0 260.5 jit_solution(7541901971706037716)
XLA Ops:
  6.5 8.3 %all-to-all-start = ((bf16[8,16,512]{2,0,1:T(8,128)(2,1)}), bf16[8,16,512]{2,0,1:T(8,128)(2,1)S(1)}, u32[]{:S(2)}, u32[]{:S(2)}) async-start(bf16[8,16,512]{2,0,1:T(8,128)(2,1)} %bitcast.27), calls=%async_computation | async-start | bytes 262144 | tf_op jit(solution)/shard_map/all_to_all | solution.py:10
  14.9 0.0 all-gather.6.cloned.1.call-start
  14.9 1.3 copy.10
  16.3 6.4 %all-to-all-done = bf16[8,16,512]{2,0,1:T(8,128)(2,1)S(1)} async-done(((bf16[8,16,512]{2,0,1:T(8,128)(2,1)}), bf16[8,16,512]{2,0,1:T(8,128)(2,1)S(1)}, u32[]{:S(2)}, u32[]{:S(2)}) %all-to-all-start) | async-done | bytes 131104 | tf_op jit(solution)/shard_map/all_to_all | solution.py:10
  22.7 28.3 %all_to_all.38 = bf16[16,512,64]{1,2,0:T(8,128)(2,1)S(1)} all-to-all(bf16[16,512,64]{1,2,0:T(8,128)(2,1)S(1)} %bitcast.23), channel_id=1, replica_groups=mesh['blk'=16,'col'=2] {'blk'}, dimensions={0} | all-to-all | bytes 2097152 | tf_op jit(solution)/shard_map/all_to_all | solution.py:11
  51.0 1.3 fusion.4
  52.3 0.0 all-gather.6.cloned.1.call-update
  52.3 0.0 all-gather.4.cloned.1.call-start
  53.0 0.7 add_divide_fusion
  53.7 111.5 %all-gather.6.cloned.1.call-done = f32[4096,1024]{1,0:T(8,128)} async-done(((f32[128,1024]{1,0:T(8,128)}), f32[4096,1024]{1,0:T(8,128)}) %all-gather.6.cloned.1.call-update) | async-done | bytes 16777232 | tf_op jit(solution)/shard_map/all_gather | solution.py:13
  165.2 7.5 %reduce_sum.9 = f32[128,1024]{1,0:T(8,128)S(1)} reduce(f32[32,128,1024]{2,1,0:T(8,128)} %bitcast.22, f32[]{:T(128)} %constant.0.clone.1), dimensions={0}, to_apply=%region_0.0 | reduce | flops 4063232 | bytes 17301508 | tf_op jit(solution)/shard_map/reduce_sum | solution.py:14
  172.6 1.3 fusion.1
  173.9 0.0 all-gather.4.cloned.1.call-update
  173.9 0.0 reduce-scatter.2.cloned.1.call-start
  174.0 59.2 %all-gather.4.cloned.1.call-done = bf16[128,8192]{1,0:T(8,128)(2,1)} async-done(((bf16[128,512]{1,0:T(8,128)(2,1)}), bf16[128,8192]{1,0:T(8,128)(2,1)}) %all-gather.4.cloned.1.call-update) | async-done | bytes 2097168 | tf_op jit(solution)/shard_map/all_gather | solution.py:18
  233.2 12.9 %fusion.6 = f32[128,1024]{1,0:T(8,128)} fusion(bf16[128,8192]{1,0:T(8,128)(2,1)} %all-gather.4.cloned.1.call-done, bf16[1024,8192]{1,0:T(8,128)(2,1)} %param.9), kind=kOutput, calls=%fused_computation.9 | convolution fusion | flops 2147483648 | bytes 19398656 | tf_op jit(solution)/shard_map/qk,nk->qn/dot_general | solution.py:19
  246.0 0.0 reduce-scatter.2.cloned.1.call-update
  246.1 6.3 %reduce-scatter.2.cloned.1.call-done = f32[64,1024]{1,0:T(8,128)} async-done(((f32[128,1024]{1,0:T(8,128)}), f32[64,1024]{1,0:T(8,128)}) %reduce-scatter.2.cloned.1.call-update) | async-done | bytes 262160 | tf_op jit(solution)/shard_map/reduce_scatter | solution.py:22
  252.3 1.6 convert_element_type.12
Async XLA Ops:
  6.5 16.1 %all-to-all-start = ((bf16[8,16,512]{2,0,1:T(8,128)(2,1)}), bf16[8,16,512]{2,0,1:T(8,128)(2,1)S(1)}, u32[]{:S(2)}, u32[]{:S(2)}) async-start(bf16[8,16,512]{2,0,1:T(8,128)(2,1)} %bitcast.27), calls=%async_computation | async-start | bytes 262144 | tf_op jit(solution)/shard_map/all_to_all | solution.py:10
  14.9 150.3 %all-gather.6.cloned.1.call-start = ((), (), s32[]{:S(2)}) async-start(), calls=%async_computation.5 | async-start | bytes 17301504 | tf_op jit(solution)/shard_map/all_gather | solution.py:13
  52.3 180.8 %all-gather.4.cloned.1.call-start = ((), (), s32[]{:S(2)}) async-start(), calls=%async_computation.3 | async-start | bytes 2228224 | tf_op jit(solution)/shard_map/all_gather | solution.py:18
  173.9 78.4 %reduce-scatter.2.cloned.1.call-start = ((), (), s32[]{:S(2)}) async-start(), calls=%async_computation.4 | async-start | bytes 786432 | tf_op jit(solution)/shard_map/reduce_scatter | solution.py:22
Sparse Core Ops, SparseCore 0:
  52.4 112.6 all-gather.5
  174.0 59.0 all-gather.3
  246.2 6.0 reduce-scatter.1
